TPU v7x, 32 devices: a whole 2x2x4 slice. The times are simulated.
32 devices in a mesh: phys: 4 (over y, x), row: 2 (over core), col: 4 (over z).
Axes of the slice: x: 2, y: 2, z: 4, core: 2. Of those that a mesh axis runs over, the one named last changes fastest.
Arguments:
- rho_sites: bfloat16 [1, 16, 2048, 2048], P(None, 'phys', 'row', 'col'), may hold values from -0.0625 to 0.0625
- sigma_sites: bfloat16 [1, 16, 2048, 2048], P(None, 'phys', 'row', 'col'), may hold values from -0.0625 to 0.0625
- environment: float32 [2048, 2048], P('row', 'col'), may hold values from -6 to 6
Outputs:
- new_environment: float32 [2048, 2048], P('row', 'col')
All inputs are finite; a program needn't handle non-finite values.
Results may differ from a plain program's by a relative error of at most 0.004.
Values may be sent and summed in bfloat16 or wider, within the bound.
A program may use at most 128 MiB of HBM per device.

v0:
```python
import jax
import jax.numpy as jnp
from jax import lax
from jax.sharding import PartitionSpec as P


def per_device(rho_sites, sigma_sites, environment):
    env = environment
    rho_block = rho_sites[0]
    sigma_block = sigma_sites[0]
    env_b = env.astype(jnp.bfloat16)
    env_whole = lax.all_gather(env_b, "col", axis=1, tiled=True)
    half = jnp.einsum(
        "ik,pkl->pil",
        env_whole,
        lax.all_gather(sigma_block, "row", axis=1, tiled=True),
        preferred_element_type=jnp.float32,
    ).astype(jnp.bfloat16)
    partial_env = jnp.einsum(
        "pij,pil->jl",
        lax.all_gather(rho_block, "col", axis=2, tiled=True),
        half,
        preferred_element_type=jnp.float32,
    )
    row_part = lax.psum_scatter(partial_env, "row", scatter_dimension=0, tiled=True)
    env = lax.psum(row_part, "phys")
    return env


def solution(mesh):
    placed = (P(None, "phys", "row", "col"), P(None, "phys", "row", "col"), P("row", "col"))
    return jax.shard_map(
        per_device, mesh=mesh, in_specs=placed, out_specs=P("row", "col"), check_vma=False
    )
```

profile of v0, /device:TPU:0, one launch (start us, length us, event | category | flops | bytes accessed | tf_op | source)
XLA Modules:
  0.0 524.7 jit_solution(5357533425166158105)
XLA Ops:
  6.5 0.0 all-gather.6.cloned.1.call-start
  6.5 2.7 convert_element_type.9
  9.2 0.0 all-gather.6.cloned.1.call-update
  9.3 0.0 all-gather.8.cloned.1.call-start
  9.3 0.7 all-gather.8.cloned.1.call-update
  10.0 0.0 all-gather.10.cloned.1.call-start
  10.1 0.7 all-gather.10.cloned.1.call-update
  10.7 0.0 reduce-scatter.2.cloned.1.call-start
  10.8 82.1 %all-gather.6.cloned.1.call-done = bf16[1024,2048]{1,0:T(8,128)(2,1)} async-done(((bf16[1024,512]{1,0:T(8,128)(2,1)}), bf16[1024,2048]{1,0:T(8,128)(2,1)}) %all-gather.6.cloned.1.call-update) | async-done | bytes 4194320 | tf_op jit(solution)/shard_map/all_gather | solution.py:12
  92.9 19.9 %all-gather.8.cloned.1.call-done = bf16[1,4,2048,512]{3,2,1,0:T(8,128)(2,1)} async-done(((bf16[1,4,1024,512]{3,2,1,0:T(8,128)(2,1)}), bf16[1,4,2048,512]{3,2,1,0:T(8,128)(2,1)}) %all-gather.8.cloned.1.call-update) | async-done | bytes 8388624 | tf_op jit(solution)/shard_map/all_gather | solution.py:16
  112.8 289.5 %all-gather.10.cloned.1.call-done = bf16[1,4,1024,2048]{3,2,1,0:T(8,128)(2,1)} async-done(((bf16[1,4,1024,512]{3,2,1,0:T(8,128)(2,1)}), bf16[1,4,1024,2048]{3,2,1,0:T(8,128)(2,1)}) %all-gather.10.cloned.1.call-update) | async-done | bytes 16777232 | tf_op jit(solution)/shard_map/all_gather | solution.py:21
  402.3 29.0 %fusion.15 = f32[2048,512]{0,1:T(8,128)} fusion(bf16[1,4,1024,2048]{3,2,1,0:T(8,128)(2,1)} %all-gather.10.cloned.1.call-done, bf16[1024,2048]{1,0:T(8,128)(2,1)} %all-gather.6.cloned.1.call-done, bf16[1,4,2048,512]{3,2,1,0:T(8,128)(2,1)} %all-gather.8.cloned.1.call-done), kind=kOutput, calls=%fused_computation.7 | convolution fusion | flops 17181966336 | bytes 33554432 | tf_op jit(solution)/shard_map/pij,pil->jl/dot_general | solution.py:19
  431.3 0.0 reduce-scatter.2.cloned.1.call-update
  431.3 0.0 all-reduce.2.cloned.1.call-start
  431.4 10.2 %reduce-scatter.2.cloned.1.call-done = f32[1024,512]{0,1:T(8,128)} async-done(((f32[2048,512]{0,1:T(8,128)}), f32[1024,512]{0,1:T(8,128)}) %reduce-scatter.2.cloned.1.call-update) | async-done | bytes 2097168 | tf_op jit(solution)/shard_map/reduce_scatter | solution.py:25
  441.6 0.0 all-reduce.2.cloned.1.call-update
  441.6 73.7 %all-reduce.2.cloned.1.call-done = f32[1024,512]{0,1:T(8,128)} async-done(((f32[1024,512]{0,1:T(8,128)}), f32[1024,512]{0,1:T(8,128)}) %all-reduce.2.cloned.1.call-update) | async-done | bytes 2097168 | tf_op jit(solution)/shard_map/psum | solution.py:26
  515.3 2.9 copy.4
Async XLA Ops:
  6.5 86.3 %all-gather.6.cloned.1.call-start = ((), (), s32[]{:S(2)}) async-start(), calls=%async_computation.1 | async-start | bytes 5242880 | tf_op jit(solution)/shard_map/all_gather | solution.py:12
  9.3 103.5 %all-gather.8.cloned.1.call-start = ((), (), s32[]{:S(2)}) async-start(), calls=%async_computation.4 | async-start | bytes 12582912 | tf_op jit(solution)/shard_map/all_gather | solution.py:16
  10.0 392.3 %all-gather.10.cloned.1.call-start = ((), (), s32[]{:S(2)}) async-start(), calls=%async_computation.5 | async-start | bytes 20971520 | tf_op jit(solution)/shard_map/all_gather | solution.py:21
  10.7 430.8 %reduce-scatter.2.cloned.1.call-start = ((), (), s32[]{:S(2)}) async-start(), calls=%async_computation.2 | async-start | bytes 6291456 | tf_op jit(solution)/shard_map/reduce_scatter | solution.py:25
  431.3 84.0 %all-reduce.2.cloned.1.call-start = ((), (), s32[]{:S(2)}) async-start(), calls=%async_computation.3 | async-start | bytes 4194304 | tf_op jit(solution)/shard_map/psum | solution.py:26
Sparse Core Ops, SparseCore 0:
  9.4 83.4 all-gather.5
  94.4 18.3 all-gather.7
  114.4 287.9 all-gather.9
  431.5 10.0 reduce-scatter.1
  444.5 70.7 all-reduce.1
where the time goes:
time: 525 us
  waiting for transfers between devices  477 us (91%)
  matrix products  29 us (6%)
  between operations  13.1 us (2%)
    all_gather x1, waiting for transfers between devices, per_device(): lax.all_gather(rho_block, 'col', axis=2, tiled=True)  290 us
    all_gather x1, waiting for transfers between devices, per_device(): env_whole = lax.all_gather(env_b, 'col', axis=1, tiled=True)  82.1 us
    psum x1, waiting for transfers between devices, per_device(): env = lax.psum(row_part, 'phys')  73.7 us
    dot_general x1, matrix products, per_device(): jnp.einsum('pij,pil->jl', lax.all_gather(rho_block, 'col', axis=2, tiled=...  29 us
    all_gather x1, waiting for transfers between devices, per_device(): lax.all_gather(sigma_block, 'row', axis=1, tiled=True)  19.9 us
  transfers between devices with their start and end apart: 5, of which 5 were waited for; matrix products, arithmetic and copies ran while one was open for 0% of the time, Pallas kernels for 0%

commit v1 on v0

--- a/solution.py
+++ b/solution.py
@@ -1,7 +1,15 @@
+import functools
 import jax
 import jax.numpy as jnp
 from jax import lax
 from jax.sharding import PartitionSpec as P
+
+
+def follow_things(z, peer_axis):
+    return jnp.sum(jax.lax.all_gather(z, axis_name=peer_axis), axis=0)
+
+
+detail_cube = functools.partial(follow_things, peer_axis="phys")
 
 
 def per_device(rho_sites, sigma_sites, environment):
@@ -23,7 +31,7 @@
         preferred_element_type=jnp.float32,
     )
     row_part = lax.psum_scatter(partial_env, "row", scatter_dimension=0, tiled=True)
-    env = lax.psum(row_part, "phys")
+    env = detail_cube(row_part)
     return env
 
 

time: 525 us -> 560 us (1.067)
  waiting for transfers between devices: 477 us -> 494 us
  local copies, waits for them, and re-layouts: 2.88 us -> 12.6 us
  other arithmetic: 2.69 us -> 11.2 us
    all_gather x0 -> x1, waiting for transfers between devices: none -> 90.4 us  [follow_things(): return jnp.sum(jax.lax.all_gather(z, axis_name=peer_axis), axis=0)]
    psum x1 -> x0, waiting for transfers between devices: 73.7 us -> none  [per_device(): env = lax.psum(row_part, 'phys')]
    all_gather x0 -> x1, local copies, waits for them, and re-layouts: none -> 10.8 us  [follow_things(): return jnp.sum(jax.lax.all_gather(z, axis_name=peer_axis), axis=0)]
    reduce_sum x0 -> x1, other arithmetic: none -> 8.49 us  [follow_things(): return jnp.sum(jax.lax.all_gather(z, axis_name=peer_axis), axis=0)]
where the time goes in v1:
time: 560 us
  waiting for transfers between devices  494 us (88%)
  matrix products  29.2 us (5%)
  between operations  13.1 us (2%)
  local copies, waits for them, and re-layouts  12.6 us (2%)
  other arithmetic  11.2 us (2%)
    all_gather x1, waiting for transfers between devices, per_device(): lax.all_gather(rho_block, 'col', axis=2, tiled=True)  290 us
    all_gather x1, waiting for transfers between devices, follow_things(): return jnp.sum(jax.lax.all_gather(z, axis_name=peer_axis), axis=0)  90.4 us
    all_gather x1, waiting for transfers between devices, per_device(): env_whole = lax.all_gather(env_b, 'col', axis=1, tiled=True)  82.1 us
    dot_general x1, matrix products, per_device(): jnp.einsum('pij,pil->jl', lax.all_gather(rho_block, 'col', axis=2, tiled=...  29.2 us
    all_gather x1, waiting for transfers between devices, per_device(): lax.all_gather(sigma_block, 'row', axis=1, tiled=True)  19.9 us
  transfers between devices with their start and end apart: 5, of which 5 were waited for; matrix products, arithmetic and copies ran while one was open for 0% of the time, Pallas kernels for 0%

profile of v1, /device:TPU:0, one launch (start us, length us, event | category | flops | bytes accessed | tf_op | source)
XLA Modules:
  0.0 559.9 jit_solution(1895381589218193953)
XLA Ops:
  6.5 0.0 all-gather.8.cloned.1.call-start
  6.5 2.7 convert_element_type.9
  9.2 0.0 all-gather.8.cloned.1.call-update
  9.3 0.0 all-gather.10.cloned.1.call-start
  9.3 0.7 all-gather.10.cloned.1.call-update
  10.0 0.0 all-gather.12.cloned.1.call-start
  10.1 0.7 all-gather.12.cloned.1.call-update
  10.7 0.0 reduce-scatter.2.cloned.1.call-start
  10.8 82.1 %all-gather.8.cloned.1.call-done = bf16[1024,2048]{1,0:T(8,128)(2,1)} async-done(((bf16[1024,512]{1,0:T(8,128)(2,1)}), bf16[1024,2048]{1,0:T(8,128)(2,1)}) %all-gather.8.cloned.1.call-update) | async-done | bytes 4194320 | tf_op jit(solution)/shard_map/all_gather | solution.py:20
  92.9 19.9 %all-gather.10.cloned.1.call-done = bf16[1,4,2048,512]{3,2,1,0:T(8,128)(2,1)} async-done(((bf16[1,4,1024,512]{3,2,1,0:T(8,128)(2,1)}), bf16[1,4,2048,512]{3,2,1,0:T(8,128)(2,1)}) %all-gather.10.cloned.1.call-update) | async-done | bytes 8388624 | tf_op jit(solution)/shard_map/all_gather | solution.py:24
  112.8 289.5 %all-gather.12.cloned.1.call-done = bf16[1,4,1024,2048]{3,2,1,0:T(8,128)(2,1)} async-done(((bf16[1,4,1024,512]{3,2,1,0:T(8,128)(2,1)}), bf16[1,4,1024,2048]{3,2,1,0:T(8,128)(2,1)}) %all-gather.12.cloned.1.call-update) | async-done | bytes 16777232 | tf_op jit(solution)/shard_map/all_gather | solution.py:29
  402.3 29.2 %fusion.15 = f32[2048,512]{0,1:T(8,128)} fusion(bf16[1,4,1024,2048]{3,2,1,0:T(8,128)(2,1)} %all-gather.12.cloned.1.call-done, bf16[1024,2048]{1,0:T(8,128)(2,1)} %all-gather.8.cloned.1.call-done, bf16[1,4,2048,512]{3,2,1,0:T(8,128)(2,1)} %all-gather.10.cloned.1.call-done), kind=kOutput, calls=%fused_computation.7 | convolution fusion | flops 17181966336 | bytes 33554432 | tf_op jit(solution)/shard_map/pij,pil->jl/dot_general | solution.py:27
  431.5 0.0 reduce-scatter.2.cloned.1.call-update
  431.5 0.0 all-gather.14.cloned.1.call-start
  431.6 10.2 %reduce-scatter.2.cloned.1.call-done = f32[1024,512]{0,1:T(8,128)} async-done(((f32[2048,512]{0,1:T(8,128)}), f32[1024,512]{0,1:T(8,128)}) %reduce-scatter.2.cloned.1.call-update) | async-done | bytes 2097168 | tf_op jit(solution)/shard_map/reduce_scatter | solution.py:33
  441.8 0.0 all-gather.14.cloned.1.call-update
  441.8 90.4 %all-gather.14.cloned.1.call-done = f32[4096,512]{0,1:T(8,128)} async-done(((f32[1024,512]{0,1:T(8,128)}), f32[4096,512]{0,1:T(8,128)}) %all-gather.14.cloned.1.call-update) | async-done | bytes 8388624 | tf_op jit(solution)/shard_map/all_gather | solution.py:9
  532.2 10.8 %reshape.2 = f32[4,1024,512]{1,0,2:T(4,128)} reshape(f32[4096,512]{0,1:T(8,128)} %all-gather.14.cloned.1.call-done) | data formatting | bytes 16777216 | tf_op jit(solution)/shard_map/all_gather | solution.py:9
  543.0 8.5 %reduce_sum.9 = f32[1024,512]{0,1:T(8,128)S(1)} reduce(f32[4,1024,512]{1,0,2:T(4,128)} %reshape.2, f32[]{:T(128)} %constant.0.clone.1), dimensions={0}, to_apply=%region_1.0 | reduce | flops 1572864 | bytes 10485764 | tf_op jit(solution)/shard_map/reduce_sum | solution.py:9
  551.5 1.8 copy.4
Async XLA Ops:
  6.5 86.3 %all-gather.8.cloned.1.call-start = ((), (), s32[]{:S(2)}) async-start(), calls=%async_computation.1 | async-start | bytes 5242880 | tf_op jit(solution)/shard_map/all_gather | solution.py:20
  9.3 103.5 %all-gather.10.cloned.1.call-start = ((), (), s32[]{:S(2)}) async-start(), calls=%async_computation.3 | async-start | bytes 12582912 | tf_op jit(solution)/shard_map/all_gather | solution.py:24
  10.0 392.3 %all-gather.12.cloned.1.call-start = ((), (), s32[]{:S(2)}) async-start(), calls=%async_computation.4 | async-start | bytes 20971520 | tf_op jit(solution)/shard_map/all_gather | solution.py:29
  10.7 431.0 %reduce-scatter.2.cloned.1.call-start = ((), (), s32[]{:S(2)}) async-start(), calls=%async_computation.2 | async-start | bytes 6291456 | tf_op jit(solution)/shard_map/reduce_scatter | solution.py:33
  431.5 100.7 %all-gather.14.cloned.1.call-start = ((), (), s32[]{:S(2)}) async-start(), calls=%async_computation.5 | async-start | bytes 10485760 | tf_op jit(solution)/shard_map/all_gather | solution.py:9
Sparse Core Ops, SparseCore 0:
  9.4 83.4 all-gather.7
  94.4 18.3 all-gather.9
  114.4 287.9 all-gather.11
  431.7 10.0 reduce-scatter.1
  443.5 88.7 all-gather.13
